TPU v7x, 32 devices: a whole 2x2x4 slice. The times are simulated.
32 devices in a mesh: users: 8 (over y, x, core), seq: 4 (over z).
Axes of the slice: x: 2, y: 2, z: 4, core: 2. Of those that a mesh axis runs over, the one named last changes fastest.
Arguments:
- item_table: bfloat16 [65536, 512], P(('users', 'seq')), may hold values from -6 to 6
- item_ids: int32 [8, 1536], P('users', 'seq'), may hold values from 0 to 65535, as said below
- segment_ids: int32 [8, 1536], P('users', 'seq'), may hold values from 0 to 2, never falling along the last dimension, each value on 1 to 768 neighbouring positions
- weight_in: bfloat16 [512, 2048], replicated, may hold values from -0.25 to 0.25
- weight_out: bfloat16 [512, 512], replicated, may hold values from -0.25 to 0.25
- gain_in: float32 [512], replicated, may hold values from 0.5 to 1.5
- gain_mid: float32 [512], replicated, may hold values from 0.5 to 1.5
- cotangent: bfloat16 [8, 1536, 512], P('users', 'seq'), may hold values from -6 to 6
Outputs:
- layer_out: bfloat16 [8, 1536, 512], P('users', 'seq')
- table_grad: float32 [65536, 512], P(('users', 'seq'))
- weight_in_grad: float32 [512, 2048], replicated
- weight_out_grad: float32 [512, 512], replicated
Inputs may be any that keep to these rules, and one draw needn't show every extreme that they name: `item_ids`: row r is held by device r // 2048 counted over users then seq. The 384 events of one device name rows of at most 24 events for each holding device, and in every draw each device has exactly 24 events whose rows one device holds.
All inputs are finite; a program needn't handle non-finite values.
Results may differ from a plain program's by a relative error of at most 0.006.
The roundings to bfloat16 on the way count: a program that leaves them out, or rounds other values in their place, can miss the bound.
Values may be sent and summed in bfloat16 or wider, within the bound.
A program may use at most 128 MiB of HBM per device.

v0:
```python
import jax
import jax.numpy as jnp
from jax import lax
from jax.sharding import PartitionSpec as P

HEADS = 8
HEAD_DIM = 64
epsilon = 1e-05


def normalize(values):
    centred = values - jnp.mean(values, axis=-1, keepdims=True)
    inverse = lax.rsqrt(jnp.mean(centred * centred, axis=-1, keepdims=True) + epsilon)
    return (centred * inverse, inverse)


def norm_back(grad_hat, normed, inverse):
    return inverse * (
        grad_hat
        - jnp.mean(grad_hat, axis=-1, keepdims=True)
        - normed * jnp.mean(grad_hat * normed, axis=-1, keepdims=True)
    )


def silu_slope(values):
    sigma = jax.nn.sigmoid(values)
    return sigma * (1.0 + values * (1.0 - sigma))


def split_heads(matrix):
    return matrix.reshape(matrix.shape[0], HEADS, HEAD_DIM).transpose(1, 0, 2)


def join_heads(stacked):
    return stacked.transpose(1, 0, 2).reshape(stacked.shape[1], HEADS * HEAD_DIM)


def head_scores(query, keys, visible):
    scores = jnp.einsum(
        "qd,kd->qk", query, keys, preferred_element_type=jnp.float32
    ) * HEAD_DIM ** (-0.5)
    weights = jnp.where(visible, jax.nn.silu(scores), 0.0).astype(jnp.bfloat16)
    return (scores, weights)


def score_grads(scores, upstream, values, visible):
    dweights = jnp.einsum("qd,kd->qk", upstream, values, preferred_element_type=jnp.float32)
    return (jnp.where(visible, dweights * silu_slope(scores), 0.0) * HEAD_DIM ** (-0.5)).astype(
        jnp.bfloat16
    )


def key_side(weights, dscores, head_query, head_up):
    grad_k = jnp.einsum("qk,qd->kd", dscores, head_query, preferred_element_type=jnp.float32)
    grad_v = jnp.einsum("qk,qd->kd", weights, head_up, preferred_element_type=jnp.float32)
    return (grad_k, grad_v)


def body(item_table, item_ids, segment_ids, weight_in, weight_out, gain_in, gain_mid, cotangent):
    events = item_ids[0]
    segments = segment_ids[0]
    upstream = cotangent[0]
    count = events.shape[0]
    shard_rows = item_table.shape[0]
    width = item_table.shape[1]
    devices = lax.axis_size(("users", "seq"))
    capacity = 2 * count // devices
    owner_index = events // shard_rows
    owner_hits = (owner_index[:, None] == jnp.arange(devices, dtype=jnp.int32)[None, :]).astype(
        jnp.int32
    )
    arrival = jnp.sum(jnp.cumsum(owner_hits, axis=0) * owner_hits, axis=1) - 1
    slot_of = owner_index * capacity + arrival
    wanted = jnp.zeros((devices * capacity,), jnp.int32).at[slot_of].set(events % shard_rows)
    asked = lax.all_to_all(
        wanted.reshape(devices, capacity), ("users", "seq"), split_axis=0, concat_axis=0, tiled=True
    )
    asked = asked.reshape(-1)
    served = item_table[asked]
    returned = lax.all_to_all(
        served.reshape(devices, capacity, width),
        ("users", "seq"),
        split_axis=0,
        concat_axis=0,
        tiled=True,
    )
    fetched = returned.reshape(devices * capacity, width)[slot_of]
    fetched_f = fetched.astype(jnp.float32)
    normed_in, inverse_in = normalize(fetched_f)
    normed_b = (normed_in * gain_in).astype(jnp.bfloat16)
    hidden_pre = jnp.dot(normed_b, weight_in, preferred_element_type=jnp.float32)
    hidden = jax.nn.silu(hidden_pre)
    gate_part = hidden[:, :width]
    value_b = hidden[:, width : 2 * width].astype(jnp.bfloat16)
    query_b = hidden[:, 2 * width : 3 * width].astype(jnp.bfloat16)
    key_b = hidden[:, 3 * width :].astype(jnp.bfloat16)
    key_all, value_all, segment_all = (
        lax.all_gather(key_b, "seq", axis=0, tiled=True),
        lax.all_gather(value_b, "seq", axis=0, tiled=True),
        lax.all_gather(segments, "seq", axis=0, tiled=True),
    )
    seq_rank = lax.axis_index("seq")
    local_pos = seq_rank * count + jnp.arange(count, dtype=jnp.int32)
    whole_pos = jnp.arange(key_all.shape[0], dtype=jnp.int32)
    visible = (whole_pos[None, :] <= local_pos[:, None]) & (
        segment_all[None, :] == segments[:, None]
    )

    def forward_head(triple):
        head_query, head_key, head_value = triple
        scores, weights = head_scores(head_query, head_key, visible)
        return jnp.dot(weights, head_value, preferred_element_type=jnp.float32)

    query_heads = split_heads(query_b)
    key_heads = split_heads(key_all)
    value_heads = split_heads(value_all)
    mixed = join_heads(lax.map(forward_head, (query_heads, key_heads, value_heads)))
    normed_mid, inverse_mid = normalize(mixed)
    scaled_mid = normed_mid * gain_mid
    gated = (scaled_mid * gate_part).astype(jnp.bfloat16)
    layer = (fetched_f + jnp.dot(gated, weight_out, preferred_element_type=jnp.float32)).astype(
        jnp.bfloat16
    )
    grad_wout = jnp.einsum("td,te->de", gated, upstream, preferred_element_type=jnp.float32)
    grad_gated = jnp.einsum("te,de->td", upstream, weight_out, preferred_element_type=jnp.float32)
    grad_gate = grad_gated * scaled_mid
    grad_mixed = norm_back(grad_gated * gate_part * gain_mid, normed_mid, inverse_mid).astype(
        jnp.bfloat16
    )
    upstream_heads = split_heads(grad_mixed)

    def query_head(quad):
        head_query, head_key, head_value, head_up = quad
        scores, weights = head_scores(head_query, head_key, visible)
        dscores = score_grads(scores, head_up, head_value, visible)
        return jnp.dot(dscores, head_key, preferred_element_type=jnp.float32)

    grad_query = join_heads(
        lax.map(query_head, (query_heads, key_heads, value_heads, upstream_heads))
    )
    query_all, upstream_all, segment_query = (
        lax.all_gather(query_b, "seq", axis=0, tiled=True),
        lax.all_gather(grad_mixed, "seq", axis=0, tiled=True),
        lax.all_gather(segments, "seq", axis=0, tiled=True),
    )
    seen_by = (local_pos[None, :] <= whole_pos[:, None]) & (
        segments[None, :] == segment_query[:, None]
    )

    def owner_head(quad):
        head_query, head_key, head_value, head_up = quad
        scores, weights = head_scores(head_query, head_key, seen_by)
        dscores = score_grads(scores, head_up, head_value, seen_by)
        return key_side(weights, dscores, head_query, head_up)

    stacked_k, stacked_v = lax.map(
        owner_head,
        (
            split_heads(query_all),
            split_heads(key_b),
            split_heads(value_b),
            split_heads(upstream_all),
        ),
    )
    grad_key = join_heads(stacked_k)
    grad_value = join_heads(stacked_v)
    grad_hidden = jnp.concatenate([grad_gate, grad_value, grad_query, grad_key], axis=1)
    grad_pre = (grad_hidden * silu_slope(hidden_pre)).astype(jnp.bfloat16)
    grad_win = jnp.einsum("td,tf->df", normed_b, grad_pre, preferred_element_type=jnp.float32)
    grad_normed = jnp.einsum("tf,df->td", grad_pre, weight_in, preferred_element_type=jnp.float32)
    grad_rows = norm_back(grad_normed * gain_in, normed_in, inverse_in) + upstream.astype(
        jnp.float32
    )
    weight_in_grad, weight_out_grad = lax.psum((grad_win, grad_wout), ("users", "seq"))
    outgoing = jnp.zeros((devices * capacity, width), jnp.float32).at[slot_of].set(grad_rows)
    incoming = lax.all_to_all(
        outgoing.reshape(devices, capacity, width).astype(jnp.bfloat16),
        ("users", "seq"),
        split_axis=0,
        concat_axis=0,
        tiled=True,
    ).astype(jnp.float32)
    table_grad = (
        jnp.zeros((shard_rows, width), jnp.float32)
        .at[asked]
        .add(incoming.reshape(devices * capacity, width))
    )
    return (layer[None], table_grad, weight_in_grad, weight_out_grad)


def solution(mesh):
    in_specs = (
        P(("users", "seq"), None),
        P("users", "seq"),
        P("users", "seq"),
        P(),
        P(),
        P(),
        P(),
        P("users", "seq", None),
    )
    out_specs = (P("users", "seq", None), P(("users", "seq"), None), P(), P())
    return jax.shard_map(body, mesh=mesh, in_specs=in_specs, out_specs=out_specs, check_vma=False)
```

profile of v0, /device:TPU:0, one launch (start us, length us, event | category | flops | bytes accessed | tf_op | source)
XLA Modules:
  0.0 509.7 jit_solution(5881222553301262161)
XLA Ops:
  13.0 14.3 %all_to_all.19 = s32[32,1,24]{2,1,0:T(1,128)S(1)} all-to-all(s32[32,1,24]{2,1,0:T(1,128)S(1)} %bitcast.229), channel_id=1, replica_groups=mesh['users'=8,'seq'=4] {'users','seq'}, dimensions={0} | all-to-all | bytes 6144 | tf_op jit(solution)/shard_map/all_to_all | solution.py:75
  28.7 5.2 %gather_fusion = bf16[768,512]{1,0:T(8,128)(2,1)} fusion(bf16[2048,512]{1,0:T(8,128)(2,1)} %param.14, s32[1024]{0:T(1024)S(1)} %pad_clamp_fusion.1), kind=kCustom, calls=%fused_computation | custom fusion | bytes 1575936 | tf_op jit(solution)/shard_map/gather | solution.py:79
  36.6 19.4 %all-to-all-done.1 = bf16[32,24,512]{2,1,0:T(8,128)(2,1)S(1)} async-done(((bf16[32,24,512]{2,1,0:T(8,128)(2,1)}), bf16[32,24,512]{2,1,0:T(8,128)(2,1)S(1)}, u32[]{:S(2)}, u32[]{:S(2)}) %all-to-all-start.1) | async-done | bytes 786464 | tf_op jit(solution)/shard_map/all_to_all | solution.py:80
  64.3 12.0 %all-gather = s32[1,1536]{1,0:T(1,128)S(1)} all-gather(s32[1,384]{1,0:T(1,128)S(1)} %copy-done.8), channel_id=2, replica_groups=mesh['users'=8,'seq'=4] {'seq'}, dimensions={1}, use_global_device_ids=true | all-gather | bytes 7680 | tf_op jit(solution)/shard_map/all_gather | solution.py:100
  81.7 18.9 %all-gather.6.cloned.1.call-done = bf16[1536,512]{1,0:T(8,128)(2,1)} async-done(((bf16[384,512]{1,0:T(8,128)(2,1)}), bf16[1536,512]{1,0:T(8,128)(2,1)}) %all-gather.6.cloned.1.call-update) | async-done | bytes 1572880 | tf_op jit(solution)/shard_map/all_gather | solution.py:98
  103.2 4.2 copy.54
  107.4 31.2 %all-gather.8.cloned.1.call-done = bf16[1536,512]{1,0:T(8,128)(2,1)} async-done(((bf16[384,512]{1,0:T(8,128)(2,1)}), bf16[1536,512]{1,0:T(8,128)(2,1)}) %all-gather.8.cloned.1.call-update) | async-done | bytes 1572880 | tf_op jit(solution)/shard_map/all_gather | solution.py:99
  141.3 4.2 copy.55
  145.5 19.8 %while.35 = (s32[]{:T(128)}, f32[8,384,64]{1,2,0:T(8,128)S(1)}, bf16[8,384,64]{2,1,0:T(8,128)(2,1)}, bf16[8,1536,64]{2,1,0:T(8,128)(2,1)}, bf16[8,1536,64]{2,1,0...) while((s32[]{:T(128)}, f32[8,384,64]{1,2,0:T(8,128)S(1)}, ...), condition=%wide.region_7.8_spmd.clone, body=%wide.region_6.7_spmd.clone.sunk | while | flops 156893184 | bytes 997469 | solution.py:117
  172.5 56.3 %while.37 = (s32[]{:T(128)}, f32[8,384,64]{1,2,0:T(8,128)}, bf16[8,384,64]{1,2,0:T(8,128)(2,1)}, bf16[8,1536,64]{2,1,0:T(8,128)(2,1)}, bf16[8,384,64]{2,1,0:T(8,...) while((s32[]{:T(128)}, f32[8,384,64]{1,2,0:T(8,128)}, ...), condition=%wide.region_15.16_spmd.clone, body=%wide.region_14.15_spmd.clone.sunk | while | flops 235339776 | bytes 6156389 | solution.py:139
  175.4 4.1 fusion.202
  182.4 4.2 fusion.202
  189.6 4.1 fusion.202
  196.6 4.1 fusion.202
  203.6 4.1 fusion.202
  210.7 4.1 fusion.202
  217.7 4.1 fusion.202
  224.7 4.1 fusion.202
  239.7 82.3 %while.36 = (s32[]{:T(128)}, f32[8,384,64]{1,2,0:T(8,128)}, f32[8,384,64]{1,2,0:T(8,128)}, bf16[8,1536,64]{1,2,0:T(8,128)(2,1)}, bf16[8,384,64]{1,2,0:T(8,128)(2...) while((s32[]{:T(128)}, f32[8,384,64]{1,2,0:T(8,128)}, ...), condition=%wide.region_13.14_spmd.clone, body=%wide.region_12.13_spmd.clone.sunk | while | flops 316145664 | bytes 8181869 | solution.py:156
  242.5 4.1 fusion.195
  252.8 4.1 fusion.195
  263.1 4.1 fusion.195
  273.4 4.1 fusion.195
  283.7 4.1 fusion.195
  293.9 4.1 fusion.195
  304.2 4.1 fusion.195
  314.5 4.1 fusion.195
  337.9 4.1 scatter_custom_fusion.1
  350.2 26.8 %all-to-all-done.2 = bf16[32,24,512]{2,1,0:T(8,128)(2,1)} async-done(((bf16[32,24,512]{2,1,0:T(8,128)(2,1)}), bf16[32,24,512]{2,1,0:T(8,128)(2,1)}, u32[]{:S(2)}, u32[]{:S(2)}) %all-to-all-start.2) | async-done | bytes 786464 | tf_op jit(solution)/shard_map/all_to_all | solution.py:176
  377.0 9.5 %scatter_custom_fusion.2 = f32[2048,512]{1,0:T(8,128)} fusion(s32[768]{0:T(1024)S(1)} %fusion.142, f32[]{:T(128)} %constant.117.clone.1, bf16[768,512]{1,0:T(8,128)(2,1)} %bitcast.60), kind=kCustom, calls=%fused_computation.107 | custom fusion | flops 786432 | bytes 4980740 | tf_op jit(solution)/shard_map/scatter-add | solution.py:186
  386.4 111.0 %all-reduce.3.cloned.1.call-done = (f32[512,2048]{1,0:T(8,128)}, f32[512,512]{1,0:T(8,128)}) async-done(((f32[512,2048]{1,0:T(8,128)}, f32[512,512]{1,0:T(8,128)}), (f32[512,2048]{1,0:T(8,128)}, f32[512,512]{1,0:T(8,128)})) %all-reduce.3.cloned.1.call-update) | async-done | bytes 5242896 | tf_op jit(solution)/shard_map/psum | solution.py:174
  497.4 4.8 copy.111
  (127 shorter events, 164.5 us)
Async XLA Ops:
  7.2 51.4 %copy-start = (bf16[512,2048]{1,0:T(8,128)(2,1)S(1)}, bf16[512,2048]{1,0:T(8,128)(2,1)}, u32[]{:S(2)}) copy-start(bf16[512,2048]{1,0:T(8,128)(2,1)} %param.17) | copy-start | bytes 6291460
  33.9 22.1 %all-to-all-start.1 = ((bf16[32,24,512]{2,1,0:T(8,128)(2,1)}), bf16[32,24,512]{2,1,0:T(8,128)(2,1)S(1)}, u32[]{:S(2)}, u32[]{:S(2)}) async-start(bf16[32,24,512]{2,1,0:T(8,128)(2,1)} %bitcast.219), calls=%async_computation.1 | async-start | bytes 1572864 | tf_op jit(solution)/shard_map/all_to_all | solution.py:80
  36.6 22.0 %copy-start.7 = (f32[512]{0:T(512)S(1)}, f32[512]{0:T(512)}, u32[]{:S(2)}) copy-start(f32[512]{0:T(512)} %param.19) | copy-start | bytes 6148
  36.6 64.0 %all-gather.6.cloned.1.call-start = ((), (), s32[]{:S(2)}) async-start(), calls=%async_computation.3 | async-start | bytes 1966080 | tf_op jit(solution)/shard_map/all_gather | solution.py:98
  62.5 1.8 copy-start.8
  63.5 18.2 %copy-start.3 = (bf16[384,512]{1,0:T(8,128)(2,1)}, bf16[384,512]{1,0:T(8,128)(2,1)S(1)}, u32[]{:S(2)}) copy-start(bf16[384,512]{1,0:T(8,128)(2,1)S(1)} %get-tuple-element.310) | copy-start | bytes 1179652
  63.5 75.1 %all-gather.8.cloned.1.call-start = ((), (), s32[]{:S(2)}) async-start(), calls=%async_computation.4 | async-start | bytes 1966080 | tf_op jit(solution)/shard_map/all_gather | solution.py:99
  64.3 166.9 %all-gather.12.cloned.1.call-start = ((), (), s32[]{:S(2)}) async-start(), calls=%async_computation.6 | async-start | bytes 1966080 | tf_op jit(solution)/shard_map/all_gather | solution.py:142
  81.7 153.5 %all-gather.10.cloned.1.call-start = ((), (), s32[]{:S(2)}) async-start(), calls=%async_computation.5 | async-start | bytes 1966080 | tf_op jit(solution)/shard_map/all_gather | solution.py:143
  165.3 1.5 copy-start.9
  166.8 3.2 copy-start.1
  170.3 0.9 copy-start.4
  171.2 326.1 %all-reduce.3.cloned.1.call-start = ((), (), s32[]{:S(2)}) async-start(), calls=%async_computation.7 | async-start | bytes 10485760 | tf_op jit(solution)/shard_map/psum | solution.py:174
  228.8 4.9 copy-start.5
  330.0 1.1 copy-start.2
  344.4 32.5 %all-to-all-start.2 = ((bf16[32,24,512]{2,1,0:T(8,128)(2,1)}), bf16[32,24,512]{2,1,0:T(8,128)(2,1)}, u32[]{:S(2)}, u32[]{:S(2)}) async-start(bf16[32,24,512]{2,1,0:T(8,128)(2,1)} %bitcast.223), calls=%async_computation.2 | async-start | bytes 1572864 | tf_op jit(solution)/shard_map/all_to_all | solution.py:176
  497.4 4.8 copy-start.6
Sparse Core Ops, SparseCore 0:
  63.6 36.9 all-gather.5
  102.7 35.8 all-gather.7
  140.2 35.8 all-gather.11
  178.1 35.8 all-gather.9
  334.7 162.6 all-reduce.2
where the time goes:
time: 512 us; the launch traced here: 510 us
  waiting for transfers between devices  208 us (41%)
  matrix products  176 us (34%)
  local copies, waits for them, and re-layouts  55 us (11%)
  blocking collectives  26.4 us (5%)
  other arithmetic  23.8 us (5%)
  between operations  14 us (3%)
  starting transfers between devices  6.57 us (1%)
    psum x1, waiting for transfers between devices, body(): lax.psum((grad_win, grad_wout), ('users', 'seq'))  111 us
    dot_general x16, matrix products, head_scores(): jnp.einsum('qd,kd->qk', query, keys, preferred_element_type=jnp.float32)  46.1 us
    dot_general x8, matrix products, query_head(): return jnp.dot(dscores, head_key, preferred_element_type=jnp.float32)  32.9 us
    dot_general x8, matrix products, key_side(): jnp.einsum('qk,qd->kd', dscores, head_query, preferred_element_type=jnp.f...  32.8 us
    all_gather x1, waiting for transfers between devices, body(): lax.all_gather(value_b, 'seq', axis=0, tiled=True)  31.2 us
    dot_general x8, matrix products, key_side(): jnp.einsum('qk,qd->kd', weights, head_up, preferred_element_type=jnp.floa...  26.8 us
    all_to_all x1, waiting for transfers between devices, body(): lax.all_to_all(outgoing.reshape(devices, capacity, width).astype(jnp.bflo...  26.8 us
    dot_general x8, matrix products, forward_head(): return jnp.dot(weights, head_value, preferred_element_type=jnp.float32)  19.8 us
  transfers between devices with their start and end apart: 7, of which 5 were waited for; matrix products, arithmetic and copies ran while one was open for 25% of the time, Pallas kernels for 0%

commit v1 on v0

--- a/solution.py
+++ b/solution.py
@@ -171,7 +171,7 @@
     grad_rows = norm_back(grad_normed * gain_in, normed_in, inverse_in) + upstream.astype(
         jnp.float32
     )
-    weight_in_grad, weight_out_grad = lax.psum((grad_win, grad_wout), ("users", "seq"))
+    weight_in_grad, weight_out_grad = lax.psum(lax.psum((grad_win, grad_wout), "seq"), "users")
     outgoing = jnp.zeros((devices * capacity, width), jnp.float32).at[slot_of].set(grad_rows)
     incoming = lax.all_to_all(
         outgoing.reshape(devices, capacity, width).astype(jnp.bfloat16),

time: 512 us -> 640 us (1.25)
  waiting for transfers between devices: 208 us -> 336 us
    psum x1 -> x2, waiting for transfers between devices: 111 us -> 249 us  [the longest x1 188 us: body(): lax.psum((grad_win, grad_wout), 'seq')]
    all_to_all x1, waiting for transfers between devices: 26.8 us -> 17.1 us  [body(): lax.all_to_all(outgoing.reshape(devices, capacity, width).astype(jnp.bflo...]
  transfers between devices with their start and end apart: 7 -> 8, of which waited for: 5 -> 6; matrix products, arithmetic and copies ran while one was open for 25% -> 20% of each run, Pallas kernels for 0% -> 0%
where the time goes in v1:
time: 640 us; the launch traced here: 638 us
  waiting for transfers between devices  336 us (52%)
  matrix products  176 us (28%)
  local copies, waits for them, and re-layouts  55 us (9%)
  blocking collectives  26.4 us (4%)
  other arithmetic  23.8 us (4%)
  between operations  14.4 us (2%)
  starting transfers between devices  6.63 us (1%)
    psum x1, waiting for transfers between devices, body(): lax.psum((grad_win, grad_wout), 'seq')  188 us
    psum x1, waiting for transfers between devices, body(): lax.psum(lax.psum((grad_win, grad_wout), 'seq'), 'users')  60.8 us
    dot_general x16, matrix products, head_scores(): jnp.einsum('qd,kd->qk', query, keys, preferred_element_type=jnp.float32)  46.1 us
    dot_general x8, matrix products, query_head(): return jnp.dot(dscores, head_key, preferred_element_type=jnp.float32)  32.9 us
    dot_general x8, matrix products, key_side(): jnp.einsum('qk,qd->kd', dscores, head_query, preferred_element_type=jnp.f...  32.8 us
    all_gather x1, waiting for transfers between devices, body(): lax.all_gather(value_b, 'seq', axis=0, tiled=True)  31.2 us
    dot_general x8, matrix products, key_side(): jnp.einsum('qk,qd->kd', weights, head_up, preferred_element_type=jnp.floa...  26.8 us
    dot_general x8, matrix products, forward_head(): return jnp.dot(weights, head_value, preferred_element_type=jnp.float32)  19.8 us
  transfers between devices with their start and end apart: 8, of which 6 were waited for; matrix products, arithmetic and copies ran while one was open for 20% of the time, Pallas kernels for 0%

profile of v1, /device:TPU:0, one launch (start us, length us, event | category | flops | bytes accessed | tf_op | source)
XLA Modules:
  0.0 638.0 jit_solution(3660491314754778182)
XLA Ops:
  13.0 14.3 %all_to_all.19 = s32[32,1,24]{2,1,0:T(1,128)S(1)} all-to-all(s32[32,1,24]{2,1,0:T(1,128)S(1)} %bitcast.229), channel_id=1, replica_groups=mesh['users'=8,'seq'=4] {'users','seq'}, dimensions={0} | all-to-all | bytes 6144 | tf_op jit(solution)/shard_map/all_to_all | solution.py:75
  28.7 5.2 gather_fusion
  36.6 19.4 %all-to-all-done.1 = bf16[32,24,512]{2,1,0:T(8,128)(2,1)S(1)} async-done(((bf16[32,24,512]{2,1,0:T(8,128)(2,1)}), bf16[32,24,512]{2,1,0:T(8,128)(2,1)S(1)}, u32[]{:S(2)}, u32[]{:S(2)}) %all-to-all-start.1) | async-done | bytes 786464 | tf_op jit(solution)/shard_map/all_to_all | solution.py:80
  64.3 12.0 %all-gather = s32[1,1536]{1,0:T(1,128)S(1)} all-gather(s32[1,384]{1,0:T(1,128)S(1)} %copy-done.8), channel_id=2, replica_groups=mesh['users'=8,'seq'=4] {'seq'}, dimensions={1}, use_global_device_ids=true | all-gather | bytes 7680 | tf_op jit(solution)/shard_map/all_gather | solution.py:100
  81.7 18.9 %all-gather.6.cloned.1.call-done = bf16[1536,512]{1,0:T(8,128)(2,1)} async-done(((bf16[384,512]{1,0:T(8,128)(2,1)}), bf16[1536,512]{1,0:T(8,128)(2,1)}) %all-gather.6.cloned.1.call-update) | async-done | bytes 1572880 | tf_op jit(solution)/shard_map/all_gather | solution.py:98
  103.2 4.2 copy.54
  107.4 31.2 %all-gather.8.cloned.1.call-done = bf16[1536,512]{1,0:T(8,128)(2,1)} async-done(((bf16[384,512]{1,0:T(8,128)(2,1)}), bf16[1536,512]{1,0:T(8,128)(2,1)}) %all-gather.8.cloned.1.call-update) | async-done | bytes 1572880 | tf_op jit(solution)/shard_map/all_gather | solution.py:99
  141.3 4.2 copy.55
  145.5 19.8 %while.35 = (s32[]{:T(128)}, f32[8,384,64]{1,2,0:T(8,128)S(1)}, bf16[8,384,64]{2,1,0:T(8,128)(2,1)}, bf16[8,1536,64]{2,1,0:T(8,128)(2,1)}, bf16[8,1536,64]{2,1,0...) while((s32[]{:T(128)}, f32[8,384,64]{1,2,0:T(8,128)S(1)}, ...), condition=%wide.region_7.8_spmd.clone, body=%wide.region_6.7_spmd.clone.sunk | while | flops 156893184 | bytes 997469 | solution.py:117
  172.5 56.3 %while.37 = (s32[]{:T(128)}, f32[8,384,64]{1,2,0:T(8,128)}, bf16[8,384,64]{1,2,0:T(8,128)(2,1)}, bf16[8,1536,64]{2,1,0:T(8,128)(2,1)}, bf16[8,384,64]{2,1,0:T(8,...) while((s32[]{:T(128)}, f32[8,384,64]{1,2,0:T(8,128)}, ...), condition=%wide.region_15.16_spmd.clone, body=%wide.region_14.15_spmd.clone.sunk | while | flops 235339776 | bytes 6156389 | solution.py:139
  175.4 4.1 fusion.202
  182.4 4.2 fusion.202
  189.6 4.1 fusion.202
  196.6 4.1 fusion.202
  203.6 4.1 fusion.202
  210.7 4.1 fusion.202
  217.7 4.1 fusion.202
  224.7 4.1 fusion.202
  239.7 82.3 %while.36 = (s32[]{:T(128)}, f32[8,384,64]{1,2,0:T(8,128)}, f32[8,384,64]{1,2,0:T(8,128)}, bf16[8,1536,64]{1,2,0:T(8,128)(2,1)}, bf16[8,384,64]{1,2,0:T(8,128)(2...) while((s32[]{:T(128)}, f32[8,384,64]{1,2,0:T(8,128)}, ...), condition=%wide.region_13.14_spmd.clone, body=%wide.region_12.13_spmd.clone.sunk | while | flops 316145664 | bytes 8181869 | solution.py:156
  242.5 4.1 fusion.195
  252.8 4.1 fusion.195
  263.1 4.1 fusion.195
  273.4 4.1 fusion.195
  283.7 4.1 fusion.195
  293.9 4.1 fusion.195
  304.2 4.1 fusion.195
  314.5 4.1 fusion.195
  334.6 187.8 %all-reduce.7.cloned.1.call-done = (f32[512,2048]{1,0:T(8,128)}, f32[512,512]{1,0:T(8,128)}) async-done(((f32[512,2048]{1,0:T(8,128)}, f32[512,512]{1,0:T(8,128)}), (f32[512,2048]{1,0:T(8,128)}, f32[512,512]{1,0:T(8,128)})) %all-reduce.7.cloned.1.call-update) | async-done | bytes 5242896 | tf_op jit(solution)/shard_map/psum | solution.py:174
  538.1 17.1 %all-to-all-done.2 = bf16[32,24,512]{2,1,0:T(8,128)(2,1)} async-done(((bf16[32,24,512]{2,1,0:T(8,128)(2,1)}), bf16[32,24,512]{2,1,0:T(8,128)(2,1)}, u32[]{:S(2)}, u32[]{:S(2)}) %all-to-all-start.2) | async-done | bytes 786464 | tf_op jit(solution)/shard_map/all_to_all | solution.py:176
  555.2 9.4 %scatter_custom_fusion.2 = f32[2048,512]{1,0:T(8,128)} fusion(s32[768]{0:T(1024)S(1)} %fusion.142, f32[]{:T(128)} %constant.117.clone.1, bf16[768,512]{1,0:T(8,128)(2,1)} %bitcast.60), kind=kCustom, calls=%fused_computation.107 | custom fusion | flops 786432 | bytes 4980740 | tf_op jit(solution)/shard_map/scatter-add | solution.py:186
  564.7 60.8 %all-reduce.5.cloned.1.call-done = (f32[512,2048]{1,0:T(8,128)}, f32[512,512]{1,0:T(8,128)}) async-done(((f32[512,2048]{1,0:T(8,128)}, f32[512,512]{1,0:T(8,128)}), (f32[512,2048]{1,0:T(8,128)}, f32[512,512]{1,0:T(8,128)})) %all-reduce.5.cloned.1.call-update) | async-done | bytes 5242896 | tf_op jit(solution)/shard_map/psum | solution.py:174
  625.4 4.8 copy.113
  (130 shorter events, 168.7 us)
Async XLA Ops:
  7.2 51.4 %copy-start = (bf16[512,2048]{1,0:T(8,128)(2,1)S(1)}, bf16[512,2048]{1,0:T(8,128)(2,1)}, u32[]{:S(2)}) copy-start(bf16[512,2048]{1,0:T(8,128)(2,1)} %param.17) | copy-start | bytes 6291460
  33.9 22.1 %all-to-all-start.1 = ((bf16[32,24,512]{2,1,0:T(8,128)(2,1)}), bf16[32,24,512]{2,1,0:T(8,128)(2,1)S(1)}, u32[]{:S(2)}, u32[]{:S(2)}) async-start(bf16[32,24,512]{2,1,0:T(8,128)(2,1)} %bitcast.219), calls=%async_computation.1 | async-start | bytes 1572864 | tf_op jit(solution)/shard_map/all_to_all | solution.py:80
  36.6 22.0 %copy-start.7 = (f32[512]{0:T(512)S(1)}, f32[512]{0:T(512)}, u32[]{:S(2)}) copy-start(f32[512]{0:T(512)} %param.19) | copy-start | bytes 6148
  36.6 64.0 %all-gather.6.cloned.1.call-start = ((), (), s32[]{:S(2)}) async-start(), calls=%async_computation.3 | async-start | bytes 1966080 | tf_op jit(solution)/shard_map/all_gather | solution.py:98
  62.5 1.8 copy-start.8
  63.5 18.2 %copy-start.3 = (bf16[384,512]{1,0:T(8,128)(2,1)}, bf16[384,512]{1,0:T(8,128)(2,1)S(1)}, u32[]{:S(2)}) copy-start(bf16[384,512]{1,0:T(8,128)(2,1)S(1)} %get-tuple-element.312) | copy-start | bytes 1179652
  63.5 75.1 %all-gather.8.cloned.1.call-start = ((), (), s32[]{:S(2)}) async-start(), calls=%async_computation.4 | async-start | bytes 1966080 | tf_op jit(solution)/shard_map/all_gather | solution.py:99
  64.3 166.9 %all-gather.12.cloned.1.call-start = ((), (), s32[]{:S(2)}) async-start(), calls=%async_computation.6 | async-start | bytes 1966080 | tf_op jit(solution)/shard_map/all_gather | solution.py:142
  81.7 153.5 %all-gather.10.cloned.1.call-start = ((), (), s32[]{:S(2)}) async-start(), calls=%async_computation.5 | async-start | bytes 1966080 | tf_op jit(solution)/shard_map/all_gather | solution.py:143
  165.3 1.5 copy-start.9
  166.8 3.2 copy-start.1
  170.3 0.9 copy-start.4
  171.2 351.2 %all-reduce.7.cloned.1.call-start = ((), (), s32[]{:S(2)}) async-start(), calls=%async_computation.8 | async-start | bytes 10485760 | tf_op jit(solution)/shard_map/psum | solution.py:174
  228.8 4.9 copy-start.5
  330.0 1.1 copy-start.2
  334.6 290.9 %all-reduce.5.cloned.1.call-start = ((), (), s32[]{:S(2)}) async-start(), calls=%async_computation.7 | async-start | bytes 10485760 | tf_op jit(solution)/shard_map/psum | solution.py:174
  532.4 22.8 %all-to-all-start.2 = ((bf16[32,24,512]{2,1,0:T(8,128)(2,1)}), bf16[32,24,512]{2,1,0:T(8,128)(2,1)}, u32[]{:S(2)}, u32[]{:S(2)}) async-start(bf16[32,24,512]{2,1,0:T(8,128)(2,1)} %bitcast.223), calls=%async_computation.2 | async-start | bytes 1572864 | tf_op jit(solution)/shard_map/all_to_all | solution.py:176
  625.4 4.8 copy-start.6
Sparse Core Ops, SparseCore 0:
  63.6 36.9 all-gather.5
  102.7 35.8 all-gather.7
  140.2 35.8 all-gather.11
  178.1 35.8 all-gather.9
  334.7 187.6 all-reduce.6
  525.6 99.7 all-reduce.4
